TPU v7x, 256 devices: a whole 4x4x8 slice. The times are simulated.
256 devices in a mesh: req: 32 (over z, x), row: 2 (over core), col: 4 (over y).
Axes of the slice: x: 4, y: 4, z: 8, core: 2. Of those that a mesh axis runs over, the one named last changes fastest.
Arguments:
- tokens: bfloat16 [32768, 1024], P(('req', 'row'), 'col'), may hold values from -6 to 6
- w_proj: bfloat16 [1024, 8, 512], P('col', 'row'), may hold values from -0.1875 to 0.1875
- adapter_a: bfloat16 [64, 1024, 16], P('req'), may hold values from -0.1875 to 0.1875
- adapter_b: bfloat16 [64, 16, 8, 256], P('req', None, 'row'), may hold values from -0.8984375 to 0.8984375
- adapter_row: int32 [64], replicated, may hold values from 0 to 63, each once
- adapter_of: int32 [32, 2], replicated, may hold values from 0 to 63
- len_blocks: int32 [32, 2], replicated, may hold values from 1 to 12, 16 in all within a row
- state_slot: int32 [64], replicated, may hold values from 0 to 63, as said below
- init_state: float32 [64, 8, 128, 128], P('req', 'row'), may hold values from -3 to 3
- decay: float32 [512, 8], P(('req', 'col'), 'row'), may hold values from 0 to 1, as said below
Outputs:
- memory_out: bfloat16 [32768, 1024], P(('req', 'col'), 'row')
Inputs may be any that keep to these rules, and one draw needn't show every extreme that they name: `len_blocks`: each row sums to 16. `state_slot`: a permutation of the slots; slots k * 2 to (k + 1) * 2 - 1 are those of req index k. The 2 requests of req index g take one slot of req index (g - 1) mod 32 and one of req index (g - 16) mod 32, in an order and at positions within those indices that vary by draw. `decay`: every factor is above 0 and at most 1.
All inputs are finite; a program needn't handle non-finite values.
Results may differ from a plain program's by a relative error of at most 0.0062.
Values may be sent and summed in bfloat16 or wider, within the bound.
A program may use at most 128 MiB of HBM per device.

v0:
```python
import math

import jax
import jax.numpy as jnp
from jax import lax
from jax.sharding import PartitionSpec as P

BLK = 64


def carried_in(value, axis, join, neutral):
    place = lax.axis_index(axis)
    gathered = jax.tree.map(
        lambda a, kind: lax.all_gather(a.astype(kind), axis),
        value,
        jax.tree.map(lambda a: jnp.bfloat16 if a.dtype == jnp.float32 else a.dtype, value),
    )
    state = jax.tree.map(lambda a, e: jnp.zeros_like(a) + jnp.asarray(e, a.dtype), value, neutral)

    def one(lap, state):
        return join(
            state,
            jax.tree.map(
                lambda a, own: lax.dynamic_index_in_dim(a, lap, 0, False).astype(own.dtype),
                gathered,
                value,
            ),
        )

    return lax.fori_loop(0, place, one, state)


def unit(values):
    scale = lax.rsqrt(jnp.mean(values * values, axis=-1, keepdims=True) + 1e-06)
    return values * scale / math.sqrt(values.shape[-1])


def block_info(lengths, block_ids):
    starts = jnp.cumsum(lengths) - lengths
    is_start = jnp.any(block_ids[:, None] == starts[None, :], axis=1)
    request = jnp.sum((block_ids[:, None] >= starts[None, :]).astype(jnp.int32), axis=1) - 1
    return (is_start, request)


def add_adapter(base_part, delta):
    return jnp.stack(
        [
            base_part[:, :, 0] + delta[:, :, 0],
            base_part[:, :, 1],
            base_part[:, :, 2] + delta[:, :, 1],
            base_part[:, :, 3],
        ],
        axis=2,
    )


def compose(earlier, later):
    return (earlier[0] * later[0], later[0][:, None, None] * earlier[1] + later[1])


def body(
    tokens,
    w_proj,
    adapter_a,
    adapter_b,
    adapter_row,
    adapter_of,
    len_blocks,
    state_slot,
    init_state,
    decay,
):
    highest = lax.Precision.HIGHEST
    group_id = lax.axis_index("req")
    column = lax.axis_index("col")
    n_col = lax.axis_size("col")
    width = adapter_a.shape[1]
    rank = adapter_a.shape[2]
    req_grp = adapter_of.shape[1]
    heads_here = w_proj.shape[1]
    head_dim = w_proj.shape[2] // 4
    slice_width = tokens.shape[1]
    gathered = lax.all_gather(tokens, "row", axis=0, tiled=True)
    group_tok = gathered.shape[0]
    own_count = group_tok // n_col
    nblk_group = group_tok // BLK
    nblk_here = own_count // BLK
    block_ids = jnp.arange(nblk_group, dtype=jnp.int32)
    is_start, request = block_info(len_blocks[group_id], block_ids)
    onehot = (
        jnp.repeat(request, BLK)[:, None] == jnp.arange(req_grp, dtype=jnp.int32)[None, :]
    ).astype(jnp.float32)
    picked = adapter_row[adapter_of[group_id]]
    table_a, table_b = (
        lax.all_gather(adapter_a, "req", axis=0, tiled=True),
        lax.all_gather(adapter_b, "req", axis=0, tiled=True),
    )
    chosen_a = table_a[picked]
    chosen_b = table_b[picked]
    a_stack = jnp.transpose(chosen_a, (1, 0, 2)).reshape(width, req_grp * rank)
    b_stack = chosen_b.reshape(req_grp * rank, heads_here * 2 * head_dim).astype(jnp.float32)
    w_flat = w_proj.reshape(w_proj.shape[0], heads_here * 4 * head_dim)
    a_part = lax.dynamic_slice_in_dim(a_stack, column * slice_width, slice_width, 0)
    count = own_count * lax.axis_size("col")
    projected = jnp.dot(gathered, w_flat, preferred_element_type=jnp.float32)
    lowrank = jnp.dot(gathered, a_part, preferred_element_type=jnp.float32).reshape(
        count, req_grp, rank
    )
    lowrank = (lowrank * onehot[:, :, None]).reshape(count, req_grp * rank)
    delta = jnp.dot(lowrank, b_stack, precision=highest)
    joined = add_adapter(
        projected.reshape(count, heads_here, 4, head_dim),
        delta.reshape(count, heads_here, 2, head_dim),
    )
    summed = lax.psum_scatter(
        joined.reshape(count, heads_here * 4 * head_dim), "col", scatter_dimension=0, tiled=True
    )
    parts = summed.reshape(own_count, heads_here, 4, head_dim).astype(jnp.bfloat16)
    here_start = lax.dynamic_slice_in_dim(is_start, column * nblk_here, nblk_here, 0)
    here_request = lax.dynamic_slice_in_dim(request, column * nblk_here, nblk_here, 0)
    state_table = lax.all_gather(init_state, "req", axis=0, tiled=True)
    state_index = state_slot[group_id * req_grp + here_request]
    query = unit(parts[:, :, 0].astype(jnp.float32)).reshape(nblk_here, BLK, heads_here, head_dim)
    keys_n = unit(parts[:, :, 1].astype(jnp.float32)).reshape(nblk_here, BLK, heads_here, head_dim)
    values = parts[:, :, 2].astype(jnp.float32).reshape(nblk_here, BLK, heads_here, head_dim)
    causal = jnp.tril(jnp.ones((BLK, BLK), jnp.float32))

    def step(carry, blocks):
        amount, state = carry
        q_block, k_block, v_block, fade, start_here, slot = blocks
        amount = jnp.where(start_here, jnp.zeros_like(amount), amount)
        state = jnp.where(start_here, state_table[slot], state)
        read = jnp.einsum("thd,hde->the", q_block, state, precision=highest)
        scores = jnp.einsum("thd,shd->hts", q_block, k_block, precision=highest) * causal[None]
        inner = jnp.einsum("hts,she->the", scores, v_block, precision=highest)
        update = jnp.einsum("thd,the->hde", k_block, v_block, precision=highest) / BLK
        return ((fade * amount, fade[:, None, None] * state + update), (read + inner, amount))

    start_carry = (
        jnp.ones((heads_here,), jnp.float32),
        jnp.zeros((heads_here, head_dim, head_dim), jnp.float32),
    )
    last_carry, (local_mem, amounts) = lax.scan(
        step, start_carry, (query, keys_n, values, decay, here_start, state_index)
    )
    identity = (
        jnp.ones((heads_here,), jnp.float32),
        jnp.zeros((heads_here, head_dim, head_dim), jnp.float32),
    )
    incoming = carried_in(last_carry, "col", compose, identity)
    carried = jnp.einsum("nthd,hde->nthe", query, incoming[1], precision=highest)
    mem = local_mem + carried * amounts[:, None, :, None]
    gate_part = parts[:, :, 3].astype(jnp.float32)
    result = jax.nn.sigmoid(gate_part) * mem.reshape(own_count, heads_here, head_dim)
    return result.reshape(own_count, heads_here * head_dim).astype(jnp.bfloat16)


def solution(mesh):
    placed = (
        P(("req", "row"), "col"),
        P("col", "row", None),
        P("req", None, None),
        P("req", None, "row", None),
        P(),
        P(),
        P(),
        P(),
        P("req", "row", None, None),
        P(("req", "col"), "row"),
    )
    return jax.shard_map(
        body, mesh=mesh, in_specs=placed, out_specs=P(("req", "col"), "row"), check_vma=False
    )
```

profile of v0, /device:TPU:25, one launch (start us, length us, event | category | flops | bytes accessed | tf_op | source)
XLA Modules:
  0.0 464.7 jit_solution(1949894486857903738)
XLA Ops:
  6.5 1.5 copy.67
  8.1 0.7 all-gather.6.cloned.1.call-update
  8.9 0.9 dynamic-slice_reduce_fusion
  10.1 1.5 copy.92
  11.7 0.5 copy.66
  12.3 0.6 gather_fusion
  12.9 2.5 all_gather.24
  15.4 4.5 fusion.29
  19.9 66.0 %all-gather.8.cloned.1.call-done = bf16[64,16,4,256]{3,1,2,0:T(8,128)(2,1)} async-done(((bf16[2,16,4,256]{3,1,2,0:T(8,128)(2,1)}), bf16[64,16,4,256]{3,1,2,0:T(8,128)(2,1)}) %all-gather.8.cloned.1.call-update) | async-done | bytes 2097168 | tf_op jit(solution)/shard_map/all_gather | solution.py:96
  85.9 2.1 gather_fusion.2
  88.2 75.5 %all-gather.6.cloned.1.call-done = bf16[64,1024,16]{1,2,0:T(8,128)(2,1)} async-done(((bf16[2,1024,16]{1,2,0:T(8,128)(2,1)}), bf16[64,1024,16]{1,2,0:T(8,128)(2,1)}) %all-gather.6.cloned.1.call-update) | async-done | bytes 2097168 | tf_op jit(solution)/shard_map/all_gather | solution.py:95
  163.7 2.1 gather_fusion.1
  166.1 1.9 fusion.32
  168.0 5.0 %slice_add_fusion.1 = (f32[1024,4,1,128]{0,3,2,1:T(8,128)S(1)}, f32[1024,4,1,128]{0,3,2,1:T(8,128)S(1)}, f32[1024,4,1,128]{0,3,2,1:T(8,128)S(1)}, f32[1024,4,1,128]{0,3,2,1:T(8,128)S(1)}) fusion(f32[1024,4,2,128]{0,3,2,1:T(8,128)S(1)} %fusion.32, f32[1024,4,4,128]{0,3,2,1:T(8,128)} %fusion.29), kind=kLoop, calls=%fused_computation.42 | loop fusion | flops 1048576 | bytes 20971520 | tf_op jit(solution)/shard_map/add | solution.py:48
  173.0 3.6 pad_maximum_fusion
  176.7 0.5 all-gather.10.cloned.1.call-update
  177.5 0.6 gather_fusion.3
  178.1 0.6 dynamic-slice
  179.4 80.4 %reduce-scatter.2.cloned.1.call-done = f32[256,2048]{0,1:T(8,128)} async-done(((f32[1024,2048]{0,1:T(8,128)}), f32[256,2048]{0,1:T(8,128)}) %reduce-scatter.2.cloned.1.call-update) | async-done | bytes 2097168 | tf_op jit(solution)/shard_map/reduce_scatter | solution.py:115
  259.8 1.7 convert_element_type.78
  263.1 139.8 %all-gather.10.cloned.1.call-done = f32[64,4,128,128]{3,2,1,0:T(8,128)} async-done(((f32[2,4,128,128]{3,2,1,0:T(8,128)}), f32[64,4,128,128]{3,2,1,0:T(8,128)}) %all-gather.10.cloned.1.call-update) | async-done | bytes 16777232 | tf_op jit(solution)/shard_map/all_gather | solution.py:121
  402.9 35.4 %while.30 = (s32[]{:T(128)}, f32[4]{0:T(128)S(1)}, f32[4,128,128]{2,1,0:T(8,128)S(1)}, f32[4,64,4,128]{3,1,0,2:T(8,128)S(1)}, f32[4,4]{1,0:T(4,128)S(1)}, /*inde...) while((s32[]{:T(128)}, f32[4]{0:T(128)S(1)}, ...), condition=%wide.region_7.8_spmd.clone, body=%wide.region_6.7_spmd.clone.sunk | while | flops 151511056 | bytes 2741074 | solution.py:143
  402.9 0.6 dynamic_slice.124
  405.8 0.6 dynamic_slice.123
  406.4 1.9 fusion.70
  408.3 1.3 fusion.66
  409.6 2.1 fusion.67
  411.7 0.6 dynamic_slice.124
  414.7 0.6 dynamic_slice.123
  415.3 1.9 fusion.70
  417.1 1.3 fusion.66
  418.4 2.1 fusion.67
  420.6 0.6 dynamic_slice.124
  423.5 0.6 dynamic_slice.123
  424.1 1.9 fusion.70
  426.0 1.3 fusion.66
  427.2 2.1 fusion.67
  429.4 0.6 dynamic_slice.124
  432.4 0.6 dynamic_slice.123
  433.0 1.9 fusion.70
  434.8 1.3 fusion.66
  436.1 2.1 fusion.67
  438.6 10.1 %all-gather.1 = bf16[16,128,128]{2,1,0:T(8,128)(2,1)S(1)} all-gather(bf16[4,128,128]{2,1,0:T(8,128)(2,1)S(1)} %convert_element_type.90), channel_id=3, replica_groups=mesh['req'=32,'row'=2,'col'=4] {'col'}, dimensions={0}, use_global_device_ids=true | all-gather | bytes 655360 | tf_op jit(solution)/shard_map/all_gather | solution.py:14
  448.7 6.2 %all-reduce = bf16[16]{0:T(256)(128)(2,1)S(1)} all-reduce(bf16[16]{0:T(256)(128)(2,1)S(1)} %dynamic-update-slice), channel_id=2, replica_groups=mesh['req'=32,'row'=2,'col'=4] {'col'}, use_global_device_ids=true, to_apply=%add | all-reduce | flops 16 | bytes 64
  454.9 0.5 while.29
  455.5 0.6 fusion.40
  456.6 0.6 reshape.221
  457.4 0.8 copy.80
  (83 shorter events, 6.8 us)
Async XLA Ops:
  6.5 171.0 %copy-start = (s32[64]{0:T(128)S(1)}, s32[64]{0:T(128)}, u32[]{:S(2)}) copy-start(s32[64]{0:T(128)} %param.21) | copy-start | bytes 772
  6.5 79.4 %all-gather.8.cloned.1.call-start = ((), (), s32[]{:S(2)}) async-start(), calls=%async_computation.2 | async-start | bytes 2162688 | tf_op jit(solution)/shard_map/all_gather | solution.py:96
  8.1 155.6 %all-gather.6.cloned.1.call-start = ((), (), s32[]{:S(2)}) async-start(), calls=%async_computation.1 | async-start | bytes 2162688 | tf_op jit(solution)/shard_map/all_gather | solution.py:95
  8.8 251.0 %reduce-scatter.2.cloned.1.call-start = ((), (), s32[]{:S(2)}) async-start(), calls=%async_computation.3 | async-start | bytes 10485760 | tf_op jit(solution)/shard_map/reduce_scatter | solution.py:115
  10.1 2.1 copy-start.1
  10.1 2.8 copy-start.3
  176.6 1.5 copy-start.4
  176.6 226.3 %all-gather.10.cloned.1.call-start = ((), (), s32[]{:S(2)}) async-start(), calls=%async_computation.4 | async-start | bytes 17301504 | tf_op jit(solution)/shard_map/all_gather | solution.py:121
  262.1 140.7 %copy-start.2 = (f32[4,64,4,128]{3,1,0,2:T(8,128)S(1)}, f32[4,64,4,128]{3,1,0,2:T(8,128)}, u32[]{:S(2)}) copy-start(f32[4,64,4,128]{3,1,0,2:T(8,128)} %custom-call.10) | copy-start | bytes 1572868
Sparse Core Ops, SparseCore 0:
  9.9 75.9 all-gather.7
  88.5 75.1 all-gather.5
  176.7 83.0 reduce-scatter.1
  262.2 140.6 all-gather.9
where the time goes:
time: 472 us; the launch traced here: 465 us
  waiting for transfers between devices  363 us (77%)
  matrix products  25.8 us (5%)
  local copies, waits for them, and re-layouts  18.8 us (4%)
  blocking collectives  18.7 us (4%)
  other arithmetic  17.2 us (4%)
  between operations  14 us (3%)
  loops' own time  7.04 us (1%)
    all_gather x1, waiting for transfers between devices, body(): state_table = lax.all_gather(init_state, 'req', axis=0, tiled=True)  140 us
    reduce_scatter x1, waiting for transfers between devices, body(): lax.psum_scatter(joined.reshape(count, heads_here * 4 * head_dim), 'col',...  80.4 us
    all_gather x1, waiting for transfers between devices, body(): lax.all_gather(adapter_a, 'req', axis=0, tiled=True)  75.5 us
    all_gather x1, waiting for transfers between devices, body(): lax.all_gather(adapter_b, 'req', axis=0, tiled=True)  66 us
    all_gather x1, blocking collectives, carried_in(): lax.all_gather(a.astype(kind), axis)  10.1 us
  transfers between devices with their start and end apart: 4, of which 4 were waited for; matrix products, arithmetic and copies ran while one was open for 3% of the time, Pallas kernels for 0%

commit v1 on v0

v1 whole, which is shorter than its diff:
```python
import functools
import math

import jax
import jax.numpy as jnp
from jax import lax
from jax.experimental import pallas as pl
from jax.experimental.pallas import tpu as pltpu
from jax.sharding import PartitionSpec as P

BLK = 64
NX = 4
NY = 4
MESH = pl.DeviceIdType.MESH
F32 = jnp.float32
BF16 = jnp.bfloat16


def kernel(
    n_req,
    row_ref,
    of_ref,
    len_ref,
    slot_ref,
    tok_ref,
    w_ref,
    a_ref,
    b_ref,
    state_ref,
    decay_ref,
    out_ref,
    tok,
    w,
    za,
    zb,
    xsa,
    xsb,
    xra,
    xrb,
    afull,
    bfull,
    bh,
    states,
    dec,
    carry,
    osend,
    tok_s,
    tok_r,
    w_s,
    w_r,
    z_s,
    z_r,
    x_s,
    x_r,
    g_s,
    g_r,
    st_s,
    st_r,
    d_s,
    d_r,
    o_s,
    o_r,
    loc,
):
    nz = n_req // NX
    g = lax.axis_index("req")
    r = lax.axis_index("row")
    c = lax.axis_index("col")
    z, x = g // NX, lax.rem(g, NX)
    sib = 1 - r
    right, left, opp = lax.rem(c + 1, NY), lax.rem(c + 3, NY), lax.rem(c + 2, NY)
    half = tok_ref.shape[0]
    part = half // 2
    base = r * half

    def rem_copy(src, dst, ssem, rsem, dev):
        return pltpu.make_async_remote_copy(
            src_ref=src, dst_ref=dst, send_sem=ssem, recv_sem=rsem, device_id=dev, device_id_type=MESH
        )

    def at_z(d):
        return {"req": lax.rem(z + d, nz) * NX + x}

    def at_x(d):
        return {"req": z * NX + lax.rem(x + d, NX)}

    def at_g(d):
        return {"req": lax.rem(g + d, n_req)}

    group = [(dr, dc) for dr in range(2) for dc in range(NY) if dr or dc]

    def in_group(dr, dc):
        return {"row": lax.rem(r + dr, 2), "col": lax.rem(c + dc, NY)}

    barrier = pltpu.get_barrier_semaphore()
    partners = [in_group(*p) for p in group]
    partners += [at_z(d) for d in range(1, nz)] + [at_x(d) for d in range(1, NX)]
    partners += [at_g(1), at_g(n_req - 1)]
    for dev in partners:
        pl.semaphore_signal(barrier, inc=1, device_id=dev, device_id_type=MESH)
    pl.semaphore_wait(barrier, len(partners))

    f = 2 * c + r
    fa = pl.multiple_of(f * 128, 128)
    mine_a = a_ref.at[:, :, pl.ds(fa, 128)]
    mine_b = b_ref.at[:, pl.ds(4 * c, 4)]
    sends = []
    z_in = []
    for d in range(1, nz):
        for k, (src, dst) in enumerate(((mine_a, za), (mine_b, zb))):
            cp = rem_copy(src, dst.at[pl.ds(2 * z, 2)], z_s.at[k, d], z_r.at[k, d], at_z(d))
            cp.start()
            sends.append(cp)
            zo = lax.rem(z + nz - d, nz)
            slot = dst.at[pl.ds(2 * zo, 2)]
            z_in.append(rem_copy(src, slot, z_s.at[k, d], z_r.at[k, d], at_z(d)))
    own_a = pltpu.make_async_copy(mine_a, za.at[pl.ds(2 * z, 2)], loc.at[0])
    own_b = pltpu.make_async_copy(mine_b, zb.at[pl.ds(2 * z, 2)], loc.at[1])
    own_a.start()
    own_b.start()

    w_in = []
    for k, (to, frm) in enumerate(((right, left), (left, right), (opp, opp))):
        cp = rem_copy(w_ref.at[to], w.at[c], w_s.at[k], w_r.at[k], {"col": to})
        cp.start()
        sends.append(cp)
        w_in.append(rem_copy(w_ref.at[to], w.at[frm], w_s.at[k], w_r.at[k], {"col": to}))
    own_w = pltpu.make_async_copy(w_ref.at[c], w.at[c], loc.at[2])
    own_w.start()

    def chunk(k):
        return pl.ds(base + k * part, part)

    def tsend(i, src, dst, dev):
        cp = rem_copy(src, dst, tok_s.at[i], tok_r.at[i], dev)
        cp.start()
        sends.append(cp)

    def twait(i, slot, dev):
        rem_copy(slot, slot, tok_s.at[i], tok_r.at[i], dev).wait_recv()

    for i, (to, k) in enumerate(((right, 0), (left, 1), (right, 1), (left, 0))):
        tsend(i, tok_ref.at[pl.ds(k * part, part)], tok.at[c, chunk(k)], {"col": to})
    tsend(4, tok_ref, tok.at[c, pl.ds(base, half)], {"row": sib})
    own_t = pltpu.make_async_copy(tok_ref, tok.at[c, pl.ds(base, half)], loc.at[3])
    own_t.start()

    d_in = []
    for d in range(1, NY):
        to, frm = lax.rem(c + d, NY), lax.rem(c + NY - d, NY)
        cp = rem_copy(decay_ref, dec.at[c], d_s.at[d], d_r.at[d], {"col": to})
        cp.start()
        sends.append(cp)
        d_in.append(rem_copy(decay_ref, dec.at[frm], d_s.at[d], d_r.at[d], {"col": to}))
    own_d = pltpu.make_async_copy(decay_ref, dec.at[c], loc.at[4])
    own_d.start()
    st_in = []
    for k, d in enumerate((1, n_req // 2)):
        cp = rem_copy(state_ref.at[:, c], states.at[pl.ds(2 * k, 2)], st_s.at[k], st_r.at[k], at_g(d))
        cp.start()
        sends.append(cp)
        st_in.append(cp)

    slot_l0, slot_l1 = tok.at[left, chunk(0)], tok.at[left, chunk(1)]
    slot_r0, slot_r1 = tok.at[right, chunk(0)], tok.at[right, chunk(1)]
    slot_o0, slot_o1 = tok.at[opp, chunk(0)], tok.at[opp, chunk(1)]
    twait(0, slot_l0, {"col": right})
    tsend(5, slot_l0, slot_l0, {"col": right})
    tsend(6, slot_l0, slot_l0, {"row": sib})
    twait(1, slot_r1, {"col": left})
    tsend(7, slot_r1, slot_r1, {"col": left})
    tsend(8, slot_r1, slot_r1, {"row": sib})

    for cp in z_in:
        cp.wait_recv()
    own_a.wait()
    own_b.wait()
    for d in range(NX):
        gx = z * NX + lax.rem(x + d, NX)
        for j in range(2):
            p = row_ref[of_ref[j, gx]]
            idx = 2 * (p // (2 * NX)) + lax.rem(p, 2)
            if d == 0:
                xra[0, j] = za[idx]
                xrb[0, j] = zb[idx]
            else:
                xsa[d - 1, j] = za[idx]
                xsb[d - 1, j] = zb[idx]
    x_in = []
    for d in range(1, NX):
        for k, (src, dst) in enumerate(((xsa, xra), (xsb, xrb))):
            cp = rem_copy(src.at[d - 1], dst.at[d], x_s.at[k, d], x_r.at[k, d], at_x(d))
            cp.start()
            sends.append(cp)
            x_in.append(cp)

    twait(2, slot_l1, {"col": right})
    tsend(9, slot_l1, slot_l1, {"row": sib})
    twait(3, slot_r0, {"col": left})
    tsend(10, slot_r0, slot_r0, {"row": sib})

    for cp in x_in:
        cp.wait_recv()
    for j in range(2):
        p = row_ref[of_ref[j, g]]
        xo = lax.rem(p // 2, NX)
        dd = lax.rem(x - xo + NX, NX)
        afull[pl.ds(16 * j, 16), pl.ds(fa, 128)] = xra[dd, j]
        bfull[j, pl.ds(4 * c, 4)] = xrb[dd, j]
    g_in = []
    ga = afull.at[:, pl.ds(fa, 128)]
    for i, (dr, dc) in enumerate(group):
        cp = rem_copy(ga, ga, g_s.at[0, i], g_r.at[0, i], in_group(dr, dc))
        cp.start()
        sends.append(cp)
        rf = 2 * lax.rem(c + NY - dc, NY) + lax.rem(r + dr, 2)
        slot = afull.at[:, pl.ds(pl.multiple_of(rf * 128, 128), 128)]
        g_in.append(rem_copy(ga, slot, g_s.at[0, i], g_r.at[0, i], in_group(dr, dc)))
        if dr == 0:
            gb = bfull.at[:, pl.ds(4 * c, 4)]
            cp = rem_copy(gb, gb, g_s.at[1, i], g_r.at[1, i], in_group(dr, dc))
            cp.start()
            sends.append(cp)
            slot = bfull.at[:, pl.ds(4 * lax.rem(c + NY - dc, NY), 4)]
            g_in.append(rem_copy(gb, slot, g_s.at[1, i], g_r.at[1, i], in_group(dr, dc)))

    twait(5, slot_o0, {"col": right})
    tsend(11, slot_o0, slot_o0, {"row": sib})
    twait(7, slot_o1, {"col": left})
    tsend(12, slot_o1, slot_o1, {"row": sib})

    other = sib * half
    own_t.wait()
    own_w.wait()
    own_d.wait()
    for cp in w_in + d_in + st_in + g_in:
        cp.wait_recv()
    dev = {"row": sib}
    twait(4, tok.at[c, pl.ds(other, half)], dev)
    twait(6, tok.at[left, pl.ds(other, part)], dev)
    twait(8, tok.at[right, pl.ds(other + part, part)], dev)
    twait(9, tok.at[left, pl.ds(other + part, part)], dev)
    twait(10, tok.at[right, pl.ds(other, part)], dev)
    twait(11, tok.at[opp, pl.ds(other, part)], dev)
    twait(12, tok.at[opp, pl.ds(other + part, part)], dev)

    head_rows = lax.broadcasted_iota(jnp.int32, (4, 256), 0) == c
    for j in range(2):
        for k in range(16):
            row = jnp.sum(jnp.where(head_rows, bfull[j, k].astype(F32), 0.0), axis=0, keepdims=True)
            bh[pl.ds(16 * j + k, 1), :] = row

    first = len_ref[0, g]
    init = []
    for j in range(2):
        s = slot_ref[2 * g + j]
        far = jnp.where(s // 2 == lax.rem(g + n_req - 1, n_req), 0, 2)
        init.append(states[far + lax.rem(s, 2)])
    carry[0] = init[0]
    carry[1] = init[1]

    tile = 4 * BLK
    rows_i = lax.broadcasted_iota(jnp.int32, (tile, 1), 0)
    ti = lax.broadcasted_iota(jnp.int32, (tile, tile), 0)
    si = lax.broadcasted_iota(jnp.int32, (tile, tile), 1)
    seen = (ti // BLK == si // BLK) & (si <= ti)
    nt = (((1,), (1,)), ((), ()))
    tn = (((0,), (0,)), ((), ()))
    inv = 1.0 / math.sqrt(128.0)

    def one_tile(m, _):
        span = pl.ds(pl.multiple_of(m * tile, tile), tile)
        proj = jnp.zeros((tile, 512), F32)
        low = jnp.zeros((tile, 32), F32)
        for cc in range(NY):
            t = tok[cc, span, :]
            proj += jnp.dot(t, w[cc], preferred_element_type=F32)
            low += lax.dot_general(t, afull[:, cc * 256 : (cc + 1) * 256], nt, preferred_element_type=F32)
        request = (m * 4 + rows_i // BLK >= first).astype(jnp.int32)
        owner = lax.broadcasted_iota(jnp.int32, (tile, 32), 1) // 16
        low = jnp.where(owner == request, low, 0.0)
        hi = low.astype(BF16)
        lo = (low - hi.astype(F32)).astype(BF16)
        up = bh[...].astype(BF16)
        delta = jnp.dot(hi, up, preferred_element_type=F32) + jnp.dot(lo, up, preferred_element_type=F32)
        q = (proj[:, 0:128] + delta[:, 0:128]).astype(BF16)
        k = proj[:, 128:256].astype(BF16)
        v = (proj[:, 256:384] + delta[:, 128:256]).astype(BF16)
        gate = proj[:, 384:512].astype(BF16).astype(F32)
        qf, kf = q.astype(F32), k.astype(F32)
        sq = lax.rsqrt(jnp.mean(qf * qf, axis=1, keepdims=True) + 1e-06) * inv
        sk = lax.rsqrt(jnp.mean(kf * kf, axis=1, keepdims=True) + 1e-06) * inv
        vk = (v.astype(F32) * sk).astype(BF16)
        scores = lax.dot_general(q, k, nt, preferred_element_type=F32)
        scores = jnp.where(seen, scores, 0.0).astype(BF16)
        inner = jnp.dot(scores, vk, preferred_element_type=F32)
        dm = dec[m]
        fade = jnp.sum(
            jnp.where(lax.broadcasted_iota(jnp.int32, (4, 4), 1) == c, dm, 0.0), axis=1, keepdims=True
        )
        reads = []
        state = carry[0]
        for i in range(4):
            state = jnp.where(m * 4 + i == first, carry[1], state)
            sl = slice(i * BLK, (i + 1) * BLK)
            reads.append(jnp.dot(q[sl], state.astype(BF16), preferred_element_type=F32))
            upd = lax.dot_general(k[sl], vk[sl], tn, preferred_element_type=F32)
            state = state * fade[i : i + 1, :] + upd * (1.0 / BLK)
        carry[0] = state
        mem = (jnp.concatenate(reads, axis=0) + inner) * sq
        osend[m] = (mem * jax.nn.sigmoid(gate)).astype(BF16)

        place = out_ref.at[:, pl.ds(pl.multiple_of(c * 128, 128), 128)]

        @pl.when(m == c)
        def _():
            pltpu.make_async_copy(osend.at[m], place, loc.at[5]).start()

        @pl.when(m != c)
        def _():
            rem_copy(osend.at[m], place, o_s.at[m], o_r.at[c], {"col": m}).start()

        return 0

    lax.fori_loop(0, NY, one_tile, 0)

    for cp in sends:
        cp.wait_send()
    for d in range(1, NY):
        frm = lax.rem(c + d, NY)
        place = out_ref.at[:, pl.ds(pl.multiple_of(frm * 128, 128), 128)]
        cp = rem_copy(osend.at[frm], place, o_s.at[frm], o_r.at[frm], {"col": frm})
        cp.wait_send()
        cp.wait_recv()
    place = out_ref.at[:, pl.ds(pl.multiple_of(c * 128, 128), 128)]
    pltpu.make_async_copy(osend.at[c], place, loc.at[5]).wait()


def body(
    n_req, tokens, w_proj, adapter_a, adapter_b, adapter_row, adapter_of, len_blocks, state_slot, init_state, decay
):
    w_heads = jnp.transpose(w_proj, (1, 0, 2))
    a_t = jnp.swapaxes(adapter_a, 1, 2)
    nz = n_req // NX
    dma = pltpu.SemaphoreType.DMA
    smem = pl.BlockSpec(memory_space=pltpu.SMEM)
    anym = pl.BlockSpec(memory_space=pl.ANY)
    return pl.pallas_call(
        functools.partial(kernel, n_req),
        out_shape=jax.ShapeDtypeStruct((256, 512), BF16),
        in_specs=[smem] * 4 + [anym] * 5 + [pl.BlockSpec(memory_space=pltpu.VMEM)],
        out_specs=anym,
        scratch_shapes=[
            pltpu.VMEM((NY, 1024, 256), BF16),
            pltpu.VMEM((NY, 256, 512), BF16),
            pltpu.VMEM((2 * nz, 16, 128), BF16),
            pltpu.VMEM((2 * nz, 4, 4, 256), BF16),
            pltpu.VMEM((NX - 1, 2, 16, 128), BF16),
            pltpu.VMEM((NX - 1, 2, 4, 4, 256), BF16),
            pltpu.VMEM((NX, 2, 16, 128), BF16),
            pltpu.VMEM((NX, 2, 4, 4, 256), BF16),
            pltpu.VMEM((32, 1024), BF16),
            pltpu.VMEM((2, 16, 4, 256), BF16),
            pltpu.VMEM((32, 256), F32),
            pltpu.VMEM((4, 128, 128), F32),
            pltpu.VMEM((NY, 4, 4), F32),
            pltpu.VMEM((2, 128, 128), F32),
            pltpu.VMEM((NY, 256, 128), BF16),
            dma((13,)),
            dma((13,)),
            dma((3,)),
            dma((3,)),
            dma((2, nz)),
            dma((2, nz)),
            dma((2, NX)),
            dma((2, NX)),
            dma((2, 7)),
            dma((2, 7)),
            dma((2,)),
            dma((2,)),
            dma((NY,)),
            dma((NY,)),
            dma((NY,)),
            dma((NY,)),
            dma((6,)),
        ],
        compiler_params=pltpu.CompilerParams(collective_id=0, has_side_effects=True),
        name="memory_layer",
    )(
        adapter_row,
        jnp.transpose(adapter_of),
        jnp.transpose(len_blocks),
        state_slot,
        tokens,
        w_heads,
        a_t,
        adapter_b,
        init_state,
        decay,
    )


def solution(mesh):
    placed = (
        P(("req", "row"), "col"),
        P("col", "row", None),
        P("req", None, None),
        P("req", None, "row", None),
        P(),
        P(),
        P(),
        P(),
        P("req", "row", None, None),
        P(("req", "col"), "row"),
    )
    return jax.shard_map(
        functools.partial(body, mesh.shape["req"]),
        mesh=mesh,
        in_specs=placed,
        out_specs=P(("req", "col"), "row"),
        check_vma=False,
    )
```

time: 472 us -> 50.6 us (0.11); the launches traced: 465 us -> 50.4 us
  waiting for transfers between devices: 363 us -> 0 us
  Pallas kernels: 0 us -> 46.3 us
  matrix products: 25.8 us -> 0 us
  blocking collectives: 18.7 us -> 0 us
  other arithmetic: 17.2 us -> 0 us
  local copies, waits for them, and re-layouts: 18.8 us -> 4.08 us
  between operations: 14 us -> 0.01 us
  loops' own time: 7.04 us -> 0 us
    all_gather x3 -> x0, waiting for transfers between devices: 281 us -> none  [the longest x1 140 us: body(): state_table = lax.all_gather(init_state, 'req', axis=0, tiled=True)]
    reduce_scatter x1 -> x0, waiting for transfers between devices: 80.4 us -> none  [body(): lax.psum_scatter(joined.reshape(count, heads_here * 4 * head_dim), 'col',...]
    pallas_call x0 -> x1, Pallas kernels: none -> 46.3 us  [body(): pl.pallas_call(functools.partial(kernel, n_req), out_shape=jax.ShapeDtype...]
    dot_general x19 -> x0, matrix products: 25.2 us -> none  [the longest x4 8.57 us: step(): jnp.einsum('thd,the->hde', k_block, v_block, precision=highest) / BLK]
    all_gather x2 -> x0, blocking collectives: 12.5 us -> none  [the longest x1 10.1 us: carried_in(): lax.all_gather(a.astype(kind), axis)]
    another operation x2 -> x0, loops' own time: 7.04 us -> none  [the longest x1 6.93 us: body(): lax.scan(step, start_carry, (query, keys_n, values, decay, here_start, st...]
    unnamed x1 -> x0, blocking collectives: 6.18 us -> none
    dynamic_slice x10 -> x0, local copies, waits for them, and re-layouts: 5.63 us -> none  [the longest x8 4.67 us: body(): lax.scan(step, start_carry, (query, keys_n, values, decay, here_start, st...]
  transfers between devices with their start and end apart: 4 -> 0, of which waited for: 4 -> 0; matrix products, arithmetic and copies ran while one was open for 3% -> 0% of each run, Pallas kernels for 0% -> 0%
where the time goes in v1:
time: 50.6 us; the launch traced here: 50.4 us
  Pallas kernels  46.3 us (92%)
  local copies, waits for them, and re-layouts  4.08 us (8%)
    pallas_call x1, Pallas kernels, body(): pl.pallas_call(functools.partial(kernel, n_req), out_shape=jax.ShapeDtype...  46.3 us
    unnamed x2, local copies, waits for them, and re-layouts  4.08 us

profile of v1, /device:TPU:25, one launch (start us, length us, event | category | flops | bytes accessed | tf_op | source)
XLA Modules:
  0.0 50.4 jit_solution(15891903874567465897)
XLA Ops:
  0.0 2.4 %copy.13 = bf16[256,4,512]{2,0,1:T(8,128)(2,1)} copy(bf16[256,4,512]{2,1,0:T(4,128)(2,1)} %param.11) | data formatting | bytes 2097152 | tf_op args[1]
  2.4 46.3 %memory_layer.1 = bf16[256,512]{1,0:T(8,128)(2,1)} custom-call(s32[64]{0:T(128)} %row_ref.1, s32[2,32]{1,0:T(2,128)} %bitcast.8, s32[2,32]{1,0:T(2,128)} %bitcast.9, s32[64]{0:T(128)} %slot_ref.1, bf16[512,256]{1,0:T(8,128)(2,1)} %tok_ref.1, bf16[4,256,512]{2,1,0:T(8,128)(2,1)} %bitcast.6, bf16[2,16,1024]{2,1,0:T(8,128)(2,1)} %bitcast.7, ...), custom_call_target="tpu_custom_call" | custom-call | tf_op jit(solution)/shard_map/memory_layer/pallas_call | solution.py:348
  48.8 1.7 %copy.15 = bf16[256,512]{1,0:T(8,128)(2,1)} copy(bf16[256,512]{1,0:T(8,128)(2,1)} %memory_layer.1) | data formatting | bytes 524288

commit v2 on v1

--- a/solution.py
+++ b/solution.py
@@ -40,6 +40,10 @@
     afull,
     bfull,
     bh,
+    wtmp,
+    acc,
+    sloc,
+    ssend,
     states,
     dec,
     carry,
@@ -61,6 +65,9 @@
     o_s,
     o_r,
     loc,
+    up_sem,
+    down_sem,
+    side_sem,
 ):
     nz = n_req // NX
     g = lax.axis_index("req")
@@ -92,74 +99,133 @@
     def in_group(dr, dc):
         return {"row": lax.rem(r + dr, 2), "col": lax.rem(c + dc, NY)}
 
+    near = [in_group(*p) for p in group] + [at_z(1), at_z(nz - 1), at_x(1), at_x(NX - 1)]
     barrier = pltpu.get_barrier_semaphore()
-    partners = [in_group(*p) for p in group]
-    partners += [at_z(d) for d in range(1, nz)] + [at_x(d) for d in range(1, NX)]
-    partners += [at_g(1), at_g(n_req - 1)]
-    for dev in partners:
+    for dev in near:
         pl.semaphore_signal(barrier, inc=1, device_id=dev, device_id_type=MESH)
-    pl.semaphore_wait(barrier, len(partners))
+    pl.semaphore_wait(barrier, len(near))
+
+    sends = []
+
+    def send(src, dst, ssem, rsem, dev):
+        cp = rem_copy(src, dst, ssem, rsem, dev)
+        cp.start()
+        sends.append(cp)
+
+    def landed(slot, ssem, rsem, dev):
+        rem_copy(slot, slot, ssem, rsem, dev).wait_recv()
+
+    hrow = lax.rem(x, 2) * 128
+    orow = 128 - hrow
+    eighth = 64
+
+    def wsend(i, src, dst, dev):
+        send(src, dst, w_s.at[i], w_r.at[i], dev)
+
+    def wwait(i, slot, dev):
+        landed(slot, w_s.at[i], w_r.at[i], dev)
+
+    mine_h = pl.ds(hrow, 128)
+    first_h, second_h = pl.ds(hrow, eighth), pl.ds(hrow + eighth, eighth)
+    first_o, second_o = pl.ds(orow, eighth), pl.ds(orow + eighth, eighth)
+    wsend(0, w_ref.at[opp, first_h], wtmp.at[0], {"col": right})
+    wsend(1, w_ref.at[opp, second_h], wtmp.at[1], {"col": left})
+    wsend(2, w_ref.at[right, mine_h], w.at[c, mine_h], {"col": right})
+    wsend(3, w_ref.at[left, mine_h], w.at[c, mine_h], {"col": left})
+
+    def chunk(k):
+        return pl.ds(base + k * part, part)
+
+    def tsend(i, src, dst, dev):
+        send(src, dst, tok_s.at[i], tok_r.at[i], dev)
+
+    def twait(i, slot, dev):
+        landed(slot, tok_s.at[i], tok_r.at[i], dev)
+
+    def tok_chunk(k):
+        return tok_ref.at[pl.ds(k * part, part)]
+
+    tsend(0, tok_chunk(0), tok.at[c, chunk(0)], {"col": right})
+    tsend(1, tok_chunk(1), tok.at[c, chunk(1)], {"col": left})
+    tsend(4, tok_ref, tok.at[c, pl.ds(base, half)], {"row": sib})
+    own_t = pltpu.make_async_copy(tok_ref, tok.at[c, pl.ds(base, half)], loc.at[3])
+    own_t.start()
+    own_w = pltpu.make_async_copy(w_ref.at[c], w.at[c], loc.at[2])
+    own_w.start()
+    own_s = pltpu.make_async_copy(state_ref.at[:, c], sloc, loc.at[6])
+    own_s.start()
+
+    d_in = []
+    for d in range(1, NY):
+        to, frm = lax.rem(c + d, NY), lax.rem(c + NY - d, NY)
+        send(decay_ref, dec.at[c], d_s.at[d], d_r.at[d], {"col": to})
+        d_in.append((dec.at[frm], d_s.at[d], d_r.at[d], {"col": to}))
+    own_d = pltpu.make_async_copy(decay_ref, dec.at[c], loc.at[4])
+    own_d.start()
+
+    for step in range(3):
+        pl.semaphore_signal(up_sem, inc=1, device_id=at_z(nz - 1), device_id_type=MESH)
+        pl.semaphore_signal(down_sem, inc=1, device_id=at_z(1), device_id_type=MESH)
+        if step == 0:
+            pl.semaphore_signal(side_sem, inc=1, device_id=at_x(NX - 1), device_id_type=MESH)
+            pl.semaphore_wait(side_sem, 1)
+        pl.semaphore_wait(up_sem, 1)
+        pl.semaphore_wait(down_sem, 1)
 
     f = 2 * c + r
     fa = pl.multiple_of(f * 128, 128)
     mine_a = a_ref.at[:, :, pl.ds(fa, 128)]
     mine_b = b_ref.at[:, pl.ds(4 * c, 4)]
-    sends = []
     z_in = []
-    for d in range(1, nz):
+    for d in (4, 3, 5, 2, 6, 1, 7):
+        zo = lax.rem(z + nz - d, nz)
         for k, (src, dst) in enumerate(((mine_a, za), (mine_b, zb))):
-            cp = rem_copy(src, dst.at[pl.ds(2 * z, 2)], z_s.at[k, d], z_r.at[k, d], at_z(d))
-            cp.start()
-            sends.append(cp)
-            zo = lax.rem(z + nz - d, nz)
-            slot = dst.at[pl.ds(2 * zo, 2)]
-            z_in.append(rem_copy(src, slot, z_s.at[k, d], z_r.at[k, d], at_z(d)))
+            send(src, dst.at[pl.ds(2 * z, 2)], z_s.at[k, d], z_r.at[k, d], at_z(d))
+            z_in.append((dst.at[pl.ds(2 * zo, 2)], z_s.at[k, d], z_r.at[k, d], at_z(d)))
     own_a = pltpu.make_async_copy(mine_a, za.at[pl.ds(2 * z, 2)], loc.at[0])
     own_b = pltpu.make_async_copy(mine_b, zb.at[pl.ds(2 * z, 2)], loc.at[1])
     own_a.start()
     own_b.start()
 
-    w_in = []
-    for k, (to, frm) in enumerate(((right, left), (left, right), (opp, opp))):
-        cp = rem_copy(w_ref.at[to], w.at[c], w_s.at[k], w_r.at[k], {"col": to})
-        cp.start()
-        sends.append(cp)
-        w_in.append(rem_copy(w_ref.at[to], w.at[frm], w_s.at[k], w_r.at[k], {"col": to}))
-    own_w = pltpu.make_async_copy(w_ref.at[c], w.at[c], loc.at[2])
-    own_w.start()
-
-    def chunk(k):
-        return pl.ds(base + k * part, part)
-
-    def tsend(i, src, dst, dev):
-        cp = rem_copy(src, dst, tok_s.at[i], tok_r.at[i], dev)
-        cp.start()
-        sends.append(cp)
-
-    def twait(i, slot, dev):
-        rem_copy(slot, slot, tok_s.at[i], tok_r.at[i], dev).wait_recv()
-
-    for i, (to, k) in enumerate(((right, 0), (left, 1), (right, 1), (left, 0))):
-        tsend(i, tok_ref.at[pl.ds(k * part, part)], tok.at[c, chunk(k)], {"col": to})
-    tsend(4, tok_ref, tok.at[c, pl.ds(base, half)], {"row": sib})
-    own_t = pltpu.make_async_copy(tok_ref, tok.at[c, pl.ds(base, half)], loc.at[3])
-    own_t.start()
-
-    d_in = []
-    for d in range(1, NY):
-        to, frm = lax.rem(c + d, NY), lax.rem(c + NY - d, NY)
-        cp = rem_copy(decay_ref, dec.at[c], d_s.at[d], d_r.at[d], {"col": to})
-        cp.start()
-        sends.append(cp)
-        d_in.append(rem_copy(decay_ref, dec.at[frm], d_s.at[d], d_r.at[d], {"col": to}))
-    own_d = pltpu.make_async_copy(decay_ref, dec.at[c], loc.at[4])
-    own_d.start()
+    own_s.wait()
     st_in = []
     for k, d in enumerate((1, n_req // 2)):
-        cp = rem_copy(state_ref.at[:, c], states.at[pl.ds(2 * k, 2)], st_s.at[k], st_r.at[k], at_g(d))
-        cp.start()
-        sends.append(cp)
-        st_in.append(cp)
+        taker = lax.rem(g + d, n_req)
+        s0, s1 = slot_ref[2 * taker], slot_ref[2 * taker + 1]
+        ssend[k] = sloc[lax.rem(jnp.where(s0 // 2 == g, s0, s1), 2)].astype(BF16)
+    for k, d in enumerate((1, n_req // 2)):
+        send(ssend.at[k], states.at[k], st_s.at[k], st_r.at[k], at_g(d))
+        st_in.append((states.at[k], st_s.at[k], st_r.at[k], at_g(d)))
+
+    wwait(0, wtmp.at[0], {"col": right})
+    wsend(4, wtmp.at[0], w.at[left, first_h], {"col": right})
+    tsend(2, tok_chunk(1), tok.at[c, chunk(1)], {"col": right})
+    wwait(1, wtmp.at[1], {"col": left})
+    wsend(5, wtmp.at[1], w.at[right, second_h], {"col": left})
+    tsend(3, tok_chunk(0), tok.at[c, chunk(0)], {"col": left})
+
+    for i, (frm, to) in enumerate(((left, right), (right, left))):
+        wwait(2 + i, w.at[frm, mine_h], {"col": to})
+        wsend(6 + 2 * i, w.at[frm, first_h], w.at[frm, first_h], at_x(1))
+        wsend(7 + 2 * i, w.at[frm, second_h], w.at[frm, second_h], at_x(NX - 1))
+
+    tile = 4 * BLK
+    other = sib * half
+    dev = {"row": sib}
+    own_t.wait()
+    own_w.wait()
+    twait(4, tok.at[c, pl.ds(other, half)], dev)
+
+    def share(q, fresh):
+        def one(m, _):
+            span = pl.ds(pl.multiple_of(m * tile, tile), tile)
+            part_sum = jnp.dot(tok[q, span, :], w[q], preferred_element_type=F32)
+            acc[span, :] = part_sum if fresh else acc[span, :] + part_sum
+            return 0
+
+        lax.fori_loop(0, NY, one, 0)
+
+    share(c, True)
 
     slot_l0, slot_l1 = tok.at[left, chunk(0)], tok.at[left, chunk(1)]
     slot_r0, slot_r1 = tok.at[right, chunk(0)], tok.at[right, chunk(1)]
@@ -171,8 +237,8 @@
     tsend(7, slot_r1, slot_r1, {"col": left})
     tsend(8, slot_r1, slot_r1, {"row": sib})
 
-    for cp in z_in:
-        cp.wait_recv()
+    for got in z_in:
+        landed(*got)
     own_a.wait()
     own_b.wait()
     for d in range(NX):
@@ -189,18 +255,21 @@
     x_in = []
     for d in range(1, NX):
         for k, (src, dst) in enumerate(((xsa, xra), (xsb, xrb))):
-            cp = rem_copy(src.at[d - 1], dst.at[d], x_s.at[k, d], x_r.at[k, d], at_x(d))
-            cp.start()
-            sends.append(cp)
-            x_in.append(cp)
+            send(src.at[d - 1], dst.at[d], x_s.at[k, d], x_r.at[k, d], at_x(d))
+            x_in.append((dst.at[d], x_s.at[k, d], x_r.at[k, d], at_x(d)))
+
+    wwait(4, w.at[opp, first_h], {"col": right})
+    wsend(10, w.at[opp, first_h], w.at[opp, first_h], at_x(1))
+    wwait(5, w.at[opp, second_h], {"col": left})
+    wsend(11, w.at[opp, second_h], w.at[opp, second_h], at_x(NX - 1))
 
     twait(2, slot_l1, {"col": right})
     tsend(9, slot_l1, slot_l1, {"row": sib})
     twait(3, slot_r0, {"col": left})
     tsend(10, slot_r0, slot_r0, {"row": sib})
 
-    for cp in x_in:
-        cp.wait_recv()
+    for got in x_in:
+        landed(*got)
     for j in range(2):
         p = row_ref[of_ref[j, g]]
         xo = lax.rem(p // 2, NX)
@@ -209,40 +278,37 @@
         bfull[j, pl.ds(4 * c, 4)] = xrb[dd, j]
     g_in = []
     ga = afull.at[:, pl.ds(fa, 128)]
+    gb = bfull.at[:, pl.ds(4 * c, 4)]
     for i, (dr, dc) in enumerate(group):
-        cp = rem_copy(ga, ga, g_s.at[0, i], g_r.at[0, i], in_group(dr, dc))
-        cp.start()
-        sends.append(cp)
-        rf = 2 * lax.rem(c + NY - dc, NY) + lax.rem(r + dr, 2)
-        slot = afull.at[:, pl.ds(pl.multiple_of(rf * 128, 128), 128)]
-        g_in.append(rem_copy(ga, slot, g_s.at[0, i], g_r.at[0, i], in_group(dr, dc)))
+        to = in_group(dr, dc)
+        fc = lax.rem(c + NY - dc, NY)
+        rf = 2 * fc + lax.rem(r + dr, 2)
+        send(ga, ga, g_s.at[0, i], g_r.at[0, i], to)
+        g_in.append((afull.at[:, pl.ds(pl.multiple_of(rf * 128, 128), 128)], g_s.at[0, i], g_r.at[0, i], to))
         if dr == 0:
-            gb = bfull.at[:, pl.ds(4 * c, 4)]
-            cp = rem_copy(gb, gb, g_s.at[1, i], g_r.at[1, i], in_group(dr, dc))
-            cp.start()
-            sends.append(cp)
-            slot = bfull.at[:, pl.ds(4 * lax.rem(c + NY - dc, NY), 4)]
-            g_in.append(rem_copy(gb, slot, g_s.at[1, i], g_r.at[1, i], in_group(dr, dc)))
+            send(gb, gb, g_s.at[1, i], g_r.at[1, i], to)
+            g_in.append((bfull.at[:, pl.ds(4 * fc, 4)], g_s.at[1, i], g_r.at[1, i], to))
+
+    for i, (frm, to) in enumerate(((left, right), (right, left))):
+        wwait(6 + 2 * i, w.at[frm, first_o], at_x(1))
+        wwait(7 + 2 * i, w.at[frm, second_o], at_x(NX - 1))
+    twait(6, tok.at[left, pl.ds(other, part)], dev)
+    twait(9, tok.at[left, pl.ds(other + part, part)], dev)
+    share(left, False)
+    twait(10, tok.at[right, pl.ds(other, part)], dev)
+    twait(8, tok.at[right, pl.ds(other + part, part)], dev)
+    share(right, False)
 
     twait(5, slot_o0, {"col": right})
     tsend(11, slot_o0, slot_o0, {"row": sib})
     twait(7, slot_o1, {"col": left})
     tsend(12, slot_o1, slot_o1, {"row": sib})
 
-    other = sib * half
-    own_t.wait()
-    own_w.wait()
     own_d.wait()
-    for cp in w_in + d_in + st_in + g_in:
-        cp.wait_recv()
-    dev = {"row": sib}
-    twait(4, tok.at[c, pl.ds(other, half)], dev)
-    twait(6, tok.at[left, pl.ds(other, part)], dev)
-    twait(8, tok.at[right, pl.ds(other + part, part)], dev)
-    twait(9, tok.at[left, pl.ds(other + part, part)], dev)
-    twait(10, tok.at[right, pl.ds(other, part)], dev)
-    twait(11, tok.at[opp, pl.ds(other, part)], dev)
-    twait(12, tok.at[opp, pl.ds(other + part, part)], dev)
+    for got in d_in + st_in + g_in:
+        landed(*got)
+    wwait(10, w.at[opp, first_o], at_x(1))
+    wwait(11, w.at[opp, second_o], at_x(NX - 1))
 
     head_rows = lax.broadcasted_iota(jnp.int32, (4, 256), 0) == c
     for j in range(2):
@@ -251,15 +317,10 @@
             bh[pl.ds(16 * j + k, 1), :] = row
 
     first = len_ref[0, g]
-    init = []
     for j in range(2):
         s = slot_ref[2 * g + j]
-        far = jnp.where(s // 2 == lax.rem(g + n_req - 1, n_req), 0, 2)
-        init.append(states[far + lax.rem(s, 2)])
-    carry[0] = init[0]
-    carry[1] = init[1]
-
-    tile = 4 * BLK
+        carry[j] = states[jnp.where(s // 2 == lax.rem(g + n_req - 1, n_req), 0, 1)].astype(F32)
+
     rows_i = lax.broadcasted_iota(jnp.int32, (tile, 1), 0)
     ti = lax.broadcasted_iota(jnp.int32, (tile, tile), 0)
     si = lax.broadcasted_iota(jnp.int32, (tile, tile), 1)
@@ -270,11 +331,10 @@
 
     def one_tile(m, _):
         span = pl.ds(pl.multiple_of(m * tile, tile), tile)
-        proj = jnp.zeros((tile, 512), F32)
+        proj = acc[span, :] + jnp.dot(tok[opp, span, :], w[opp], preferred_element_type=F32)
         low = jnp.zeros((tile, 32), F32)
         for cc in range(NY):
             t = tok[cc, span, :]
-            proj += jnp.dot(t, w[cc], preferred_element_type=F32)
             low += lax.dot_general(t, afull[:, cc * 256 : (cc + 1) * 256], nt, preferred_element_type=F32)
         request = (m * 4 + rows_i // BLK >= first).astype(jnp.int32)
         owner = lax.broadcasted_iota(jnp.int32, (tile, 32), 1) // 16
@@ -322,6 +382,8 @@
 
         return 0
 
+    twait(11, tok.at[opp, pl.ds(other, part)], dev)
+    twait(12, tok.at[opp, pl.ds(other + part, part)], dev)
     lax.fori_loop(0, NY, one_tile, 0)
 
     for cp in sends:
@@ -362,14 +424,18 @@
             pltpu.VMEM((32, 1024), BF16),
             pltpu.VMEM((2, 16, 4, 256), BF16),
             pltpu.VMEM((32, 256), F32),
-            pltpu.VMEM((4, 128, 128), F32),
+            pltpu.VMEM((2, 64, 512), BF16),
+            pltpu.VMEM((1024, 512), F32),
+            pltpu.VMEM((2, 128, 128), F32),
+            pltpu.VMEM((2, 128, 128), BF16),
+            pltpu.VMEM((2, 128, 128), BF16),
             pltpu.VMEM((NY, 4, 4), F32),
             pltpu.VMEM((2, 128, 128), F32),
             pltpu.VMEM((NY, 256, 128), BF16),
             dma((13,)),
             dma((13,)),
-            dma((3,)),
-            dma((3,)),
+            dma((12,)),
+            dma((12,)),
             dma((2, nz)),
             dma((2, nz)),
             dma((2, NX)),
@@ -382,7 +448,10 @@
             dma((NY,)),
             dma((NY,)),
             dma((NY,)),
-            dma((6,)),
+            dma((7,)),
+            pltpu.SemaphoreType.REGULAR,
+            pltpu.SemaphoreType.REGULAR,
+            pltpu.SemaphoreType.REGULAR,
         ],
         compiler_params=pltpu.CompilerParams(collective_id=0, has_side_effects=True),
         name="memory_layer",

time: 50.6 us -> 42.9 us (0.85)
  Pallas kernels: 46.3 us -> 38.6 us
    pallas_call x1, Pallas kernels: 46.3 us -> 38.6 us  [body(): pl.pallas_call(functools.partial(kernel, n_req), out_shape=jax.ShapeDtype...]
where the time goes in v2:
time: 42.9 us; the launch traced here: 42.7 us
  Pallas kernels  38.6 us (90%)
  local copies, waits for them, and re-layouts  4.08 us (10%)
    pallas_call x1, Pallas kernels, body(): pl.pallas_call(functools.partial(kernel, n_req), out_shape=jax.ShapeDtype...  38.6 us
    unnamed x2, local copies, waits for them, and re-layouts  4.08 us

profile of v2, /device:TPU:25, one launch (start us, length us, event | category | flops | bytes accessed | tf_op | source)
XLA Modules:
  0.0 42.7 jit_solution(7028059914355266431)
XLA Ops:
  0.0 2.4 %copy.13 = bf16[256,4,512]{2,0,1:T(8,128)(2,1)} copy(bf16[256,4,512]{2,1,0:T(4,128)(2,1)} %param.11) | data formatting | bytes 2097152 | tf_op args[1]
  2.4 38.6 %memory_layer.1 = bf16[256,512]{1,0:T(8,128)(2,1)} custom-call(s32[64]{0:T(128)} %row_ref.1, s32[2,32]{1,0:T(2,128)} %bitcast.8, s32[2,32]{1,0:T(2,128)} %bitcast.9, s32[64]{0:T(128)} %slot_ref.1, bf16[512,256]{1,0:T(8,128)(2,1)} %tok_ref.1, bf16[4,256,512]{2,1,0:T(8,128)(2,1)} %bitcast.6, bf16[2,16,1024]{2,1,0:T(8,128)(2,1)} %bitcast.7, ...), custom_call_target="tpu_custom_call" | custom-call | tf_op jit(solution)/shard_map/memory_layer/pallas_call | solution.py:410
  41.1 1.7 %copy.15 = bf16[256,512]{1,0:T(8,128)(2,1)} copy(bf16[256,512]{1,0:T(8,128)(2,1)} %memory_layer.1) | data formatting | bytes 524288

commit v3 on v2

--- a/solution.py
+++ b/solution.py
@@ -42,6 +42,7 @@
     bh,
     wtmp,
     acc,
+    lowacc,
     sloc,
     ssend,
     states,
@@ -329,13 +330,37 @@
     tn = (((0,), (0,)), ((), ()))
     inv = 1.0 / math.sqrt(128.0)
 
+    def low_share(q, span):
+        maps = afull[:, pl.ds(pl.multiple_of(q * 256, 256), 256)]
+        return lax.dot_general(tok[q, span, :], maps, nt, preferred_element_type=F32)
+
+    def low_three(m, _):
+        span = pl.ds(pl.multiple_of(m * tile, tile), tile)
+        lowacc[span, :] = low_share(c, span) + low_share(left, span) + low_share(right, span)
+        return 0
+
+    def last_share(m):
+        span = pl.ds(pl.multiple_of(m * tile, tile), tile)
+        acc[span, :] += jnp.dot(tok[opp, span, :], w[opp], preferred_element_type=F32)
+        lowacc[span, :] += low_share(opp, span)
+
+    lax.fori_loop(0, NY, low_three, 0)
+
+    def own_share(m, _):
+        last_share(2 * r + m)
+        return 0
+
+    lax.fori_loop(0, 2, own_share, 0)
+
     def one_tile(m, _):
+        @pl.when(m // 2 != r)
+        def _():
+            twait(11 + lax.rem(m, 2), tok.at[opp, pl.ds(pl.multiple_of(m * tile, tile), tile)], dev)
+            last_share(m)
+
         span = pl.ds(pl.multiple_of(m * tile, tile), tile)
-        proj = acc[span, :] + jnp.dot(tok[opp, span, :], w[opp], preferred_element_type=F32)
-        low = jnp.zeros((tile, 32), F32)
-        for cc in range(NY):
-            t = tok[cc, span, :]
-            low += lax.dot_general(t, afull[:, cc * 256 : (cc + 1) * 256], nt, preferred_element_type=F32)
+        proj = acc[span, :]
+        low = lowacc[span, :]
         request = (m * 4 + rows_i // BLK >= first).astype(jnp.int32)
         owner = lax.broadcasted_iota(jnp.int32, (tile, 32), 1) // 16
         low = jnp.where(owner == request, low, 0.0)
@@ -382,8 +407,6 @@
 
         return 0
 
-    twait(11, tok.at[opp, pl.ds(other, part)], dev)
-    twait(12, tok.at[opp, pl.ds(other + part, part)], dev)
     lax.fori_loop(0, NY, one_tile, 0)
 
     for cp in sends:
@@ -426,6 +449,7 @@
             pltpu.VMEM((32, 256), F32),
             pltpu.VMEM((2, 64, 512), BF16),
             pltpu.VMEM((1024, 512), F32),
+            pltpu.VMEM((1024, 32), F32),
             pltpu.VMEM((2, 128, 128), F32),
             pltpu.VMEM((2, 128, 128), BF16),
             pltpu.VMEM((2, 128, 128), BF16),

time: 42.9 us -> 43.2 us (level)
  no operation moved by 1% of the time
where the time goes in v3:
time: 43.2 us; the launch traced here: 43 us
  Pallas kernels  38.9 us (90%)
  local copies, waits for them, and re-layouts  4.08 us (9%)
    pallas_call x1, Pallas kernels, body(): pl.pallas_call(functools.partial(kernel, n_req), out_shape=jax.ShapeDtype...  38.9 us
    unnamed x2, local copies, waits for them, and re-layouts  4.08 us

profile of v3, /device:TPU:25, one launch (start us, length us, event | category | flops | bytes accessed | tf_op | source)
XLA Modules:
  0.0 43.0 jit_solution(13786761153160299282)
XLA Ops:
  0.0 2.4 %copy.13 = bf16[256,4,512]{2,0,1:T(8,128)(2,1)} copy(bf16[256,4,512]{2,1,0:T(4,128)(2,1)} %param.11) | data formatting | bytes 2097152 | tf_op args[1]
  2.4 38.9 %memory_layer.1 = bf16[256,512]{1,0:T(8,128)(2,1)} custom-call(s32[64]{0:T(128)} %row_ref.1, s32[2,32]{1,0:T(2,128)} %bitcast.8, s32[2,32]{1,0:T(2,128)} %bitcast.9, s32[64]{0:T(128)} %slot_ref.1, bf16[512,256]{1,0:T(8,128)(2,1)} %tok_ref.1, bf16[4,256,512]{2,1,0:T(8,128)(2,1)} %bitcast.6, bf16[2,16,1024]{2,1,0:T(8,128)(2,1)} %bitcast.7, ...), custom_call_target="tpu_custom_call" | custom-call | tf_op jit(solution)/shard_map/memory_layer/pallas_call | solution.py:433
  41.3 1.7 %copy.15 = bf16[256,512]{1,0:T(8,128)(2,1)} copy(bf16[256,512]{1,0:T(8,128)(2,1)} %memory_layer.1) | data formatting | bytes 524288

commit v4 on v2

--- a/solution.py
+++ b/solution.py
@@ -41,6 +41,8 @@
     bfull,
     bh,
     wtmp,
+    wraw,
+    wl,
     acc,
     sloc,
     ssend,
@@ -99,10 +101,23 @@
     def in_group(dr, dc):
         return {"row": lax.rem(r + dr, 2), "col": lax.rem(c + dc, NY)}
 
+    raw = pltpu.make_async_copy(w_ref, wraw, loc.at[7])
+    raw.start()
+
     near = [in_group(*p) for p in group] + [at_z(1), at_z(nz - 1), at_x(1), at_x(NX - 1)]
     barrier = pltpu.get_barrier_semaphore()
     for dev in near:
         pl.semaphore_signal(barrier, inc=1, device_id=dev, device_id_type=MESH)
+
+    raw.wait()
+
+    def regroup(i, _):
+        span = pl.ds(pl.multiple_of(32 * i, 32), 32)
+        for h in range(NY):
+            wl[h, span, :] = wraw[span, h, :]
+        return 0
+
+    lax.fori_loop(0, 8, regroup, 0)
     pl.semaphore_wait(barrier, len(near))
 
     sends = []
@@ -128,10 +143,10 @@
     mine_h = pl.ds(hrow, 128)
     first_h, second_h = pl.ds(hrow, eighth), pl.ds(hrow + eighth, eighth)
     first_o, second_o = pl.ds(orow, eighth), pl.ds(orow + eighth, eighth)
-    wsend(0, w_ref.at[opp, first_h], wtmp.at[0], {"col": right})
-    wsend(1, w_ref.at[opp, second_h], wtmp.at[1], {"col": left})
-    wsend(2, w_ref.at[right, mine_h], w.at[c, mine_h], {"col": right})
-    wsend(3, w_ref.at[left, mine_h], w.at[c, mine_h], {"col": left})
+    wsend(0, wl.at[opp, first_h], wtmp.at[0], {"col": right})
+    wsend(1, wl.at[opp, second_h], wtmp.at[1], {"col": left})
+    wsend(2, wl.at[right, mine_h], w.at[c, mine_h], {"col": right})
+    wsend(3, wl.at[left, mine_h], w.at[c, mine_h], {"col": left})
 
     def chunk(k):
         return pl.ds(base + k * part, part)
@@ -150,7 +165,7 @@
     tsend(4, tok_ref, tok.at[c, pl.ds(base, half)], {"row": sib})
     own_t = pltpu.make_async_copy(tok_ref, tok.at[c, pl.ds(base, half)], loc.at[3])
     own_t.start()
-    own_w = pltpu.make_async_copy(w_ref.at[c], w.at[c], loc.at[2])
+    own_w = pltpu.make_async_copy(wl.at[c], w.at[c], loc.at[2])
     own_w.start()
     own_s = pltpu.make_async_copy(state_ref.at[:, c], sloc, loc.at[6])
     own_s.start()
@@ -401,7 +416,6 @@
 def body(
     n_req, tokens, w_proj, adapter_a, adapter_b, adapter_row, adapter_of, len_blocks, state_slot, init_state, decay
 ):
-    w_heads = jnp.transpose(w_proj, (1, 0, 2))
     a_t = jnp.swapaxes(adapter_a, 1, 2)
     nz = n_req // NX
     dma = pltpu.SemaphoreType.DMA
@@ -425,6 +439,8 @@
             pltpu.VMEM((2, 16, 4, 256), BF16),
             pltpu.VMEM((32, 256), F32),
             pltpu.VMEM((2, 64, 512), BF16),
+            pltpu.VMEM((256, NY, 512), BF16),
+            pltpu.VMEM((NY, 256, 512), BF16),
             pltpu.VMEM((1024, 512), F32),
             pltpu.VMEM((2, 128, 128), F32),
             pltpu.VMEM((2, 128, 128), BF16),
@@ -448,7 +464,7 @@
             dma((NY,)),
             dma((NY,)),
             dma((NY,)),
-            dma((7,)),
+            dma((8,)),
             pltpu.SemaphoreType.REGULAR,
             pltpu.SemaphoreType.REGULAR,
             pltpu.SemaphoreType.REGULAR,
@@ -461,7 +477,7 @@
         jnp.transpose(len_blocks),
         state_slot,
         tokens,
-        w_heads,
+        w_proj,
         a_t,
         adapter_b,
         init_state,

time: 42.9 us -> 41.9 us (0.977)
  local copies, waits for them, and re-layouts: 4.08 us -> 1.67 us
  Pallas kernels: 38.6 us -> 40 us
    unnamed x2 -> x1, local copies, waits for them, and re-layouts: 4.08 us -> 1.67 us
    pallas_call x1, Pallas kernels: 38.6 us -> 40 us  [body(): pl.pallas_call(functools.partial(kernel, n_req), out_shape=jax.ShapeDtype...]
where the time goes in v4:
time: 41.9 us; the launch traced here: 41.7 us
  Pallas kernels  40 us (95%)
  local copies, waits for them, and re-layouts  1.67 us (4%)
    pallas_call x1, Pallas kernels, body(): pl.pallas_call(functools.partial(kernel, n_req), out_shape=jax.ShapeDtype...  40 us
    unnamed x1, local copies, waits for them, and re-layouts  1.67 us

profile of v4, /device:TPU:25, one launch (start us, length us, event | category | flops | bytes accessed | tf_op | source)
XLA Modules:
  0.0 41.7 jit_solution(9896419522323512946)
XLA Ops:
  0.0 40.0 %memory_layer.1 = bf16[256,512]{1,0:T(8,128)(2,1)} custom-call(s32[64]{0:T(128)} %row_ref.1, s32[2,32]{1,0:T(2,128)} %bitcast.4, s32[2,32]{1,0:T(2,128)} %bitcast.5, s32[64]{0:T(128)} %slot_ref.1, bf16[512,256]{1,0:T(8,128)(2,1)} %tok_ref.1, bf16[256,4,512]{2,1,0:T(4,128)(2,1)} %w_ref.1, bf16[2,16,1024]{2,1,0:T(8,128)(2,1)} %bitcast.3, ...), custom_call_target="tpu_custom_call" | custom-call | tf_op jit(solution)/shard_map/memory_layer/pallas_call | solution.py:424
  40.0 1.7 %copy.12 = bf16[256,512]{1,0:T(8,128)(2,1)} copy(bf16[256,512]{1,0:T(8,128)(2,1)} %memory_layer.1) | data formatting | bytes 524288

commit v5 on v4

--- a/solution.py
+++ b/solution.py
@@ -108,6 +108,58 @@
     barrier = pltpu.get_barrier_semaphore()
     for dev in near:
         pl.semaphore_signal(barrier, inc=1, device_id=dev, device_id_type=MESH)
+    pl.semaphore_wait(barrier, len(near))
+
+    sends = []
+
+    def send(src, dst, ssem, rsem, dev):
+        cp = rem_copy(src, dst, ssem, rsem, dev)
+        cp.start()
+        sends.append(cp)
+
+    def landed(slot, ssem, rsem, dev):
+        rem_copy(slot, slot, ssem, rsem, dev).wait_recv()
+
+    hrow = lax.rem(x, 2) * 128
+    orow = 128 - hrow
+    eighth = 64
+
+    def wsend(i, src, dst, dev):
+        send(src, dst, w_s.at[i], w_r.at[i], dev)
+
+    def wwait(i, slot, dev):
+        landed(slot, w_s.at[i], w_r.at[i], dev)
+
+    mine_h = pl.ds(hrow, 128)
+    first_h, second_h = pl.ds(hrow, eighth), pl.ds(hrow + eighth, eighth)
+    first_o, second_o = pl.ds(orow, eighth), pl.ds(orow + eighth, eighth)
+
+    def chunk(k):
+        return pl.ds(base + k * part, part)
+
+    def tsend(i, src, dst, dev):
+        send(src, dst, tok_s.at[i], tok_r.at[i], dev)
+
+    def twait(i, slot, dev):
+        landed(slot, tok_s.at[i], tok_r.at[i], dev)
+
+    def tok_chunk(k):
+        return tok_ref.at[pl.ds(k * part, part)]
+
+    tsend(0, tok_chunk(0), tok.at[c, chunk(0)], {"col": right})
+    tsend(1, tok_chunk(1), tok.at[c, chunk(1)], {"col": left})
+    tsend(4, tok_ref, tok.at[c, pl.ds(base, half)], {"row": sib})
+    own_t = pltpu.make_async_copy(tok_ref, tok.at[c, pl.ds(base, half)], loc.at[3])
+    own_t.start()
+    own_s = pltpu.make_async_copy(state_ref.at[:, c], sloc, loc.at[6])
+    own_s.start()
+
+    def greet():
+        pl.semaphore_signal(up_sem, inc=1, device_id=at_z(nz - 1), device_id_type=MESH)
+        pl.semaphore_signal(down_sem, inc=1, device_id=at_z(1), device_id_type=MESH)
+
+    greet()
+    pl.semaphore_signal(side_sem, inc=1, device_id=at_x(NX - 1), device_id_type=MESH)
 
     raw.wait()
 
@@ -118,57 +170,6 @@
         return 0
 
     lax.fori_loop(0, 8, regroup, 0)
-    pl.semaphore_wait(barrier, len(near))
-
-    sends = []
-
-    def send(src, dst, ssem, rsem, dev):
-        cp = rem_copy(src, dst, ssem, rsem, dev)
-        cp.start()
-        sends.append(cp)
-
-    def landed(slot, ssem, rsem, dev):
-        rem_copy(slot, slot, ssem, rsem, dev).wait_recv()
-
-    hrow = lax.rem(x, 2) * 128
-    orow = 128 - hrow
-    eighth = 64
-
-    def wsend(i, src, dst, dev):
-        send(src, dst, w_s.at[i], w_r.at[i], dev)
-
-    def wwait(i, slot, dev):
-        landed(slot, w_s.at[i], w_r.at[i], dev)
-
-    mine_h = pl.ds(hrow, 128)
-    first_h, second_h = pl.ds(hrow, eighth), pl.ds(hrow + eighth, eighth)
-    first_o, second_o = pl.ds(orow, eighth), pl.ds(orow + eighth, eighth)
-    wsend(0, wl.at[opp, first_h], wtmp.at[0], {"col": right})
-    wsend(1, wl.at[opp, second_h], wtmp.at[1], {"col": left})
-    wsend(2, wl.at[right, mine_h], w.at[c, mine_h], {"col": right})
-    wsend(3, wl.at[left, mine_h], w.at[c, mine_h], {"col": left})
-
-    def chunk(k):
-        return pl.ds(base + k * part, part)
-
-    def tsend(i, src, dst, dev):
-        send(src, dst, tok_s.at[i], tok_r.at[i], dev)
-
-    def twait(i, slot, dev):
-        landed(slot, tok_s.at[i], tok_r.at[i], dev)
-
-    def tok_chunk(k):
-        return tok_ref.at[pl.ds(k * part, part)]
-
-    tsend(0, tok_chunk(0), tok.at[c, chunk(0)], {"col": right})
-    tsend(1, tok_chunk(1), tok.at[c, chunk(1)], {"col": left})
-    tsend(4, tok_ref, tok.at[c, pl.ds(base, half)], {"row": sib})
-    own_t = pltpu.make_async_copy(tok_ref, tok.at[c, pl.ds(base, half)], loc.at[3])
-    own_t.start()
-    own_w = pltpu.make_async_copy(wl.at[c], w.at[c], loc.at[2])
-    own_w.start()
-    own_s = pltpu.make_async_copy(state_ref.at[:, c], sloc, loc.at[6])
-    own_s.start()
 
     d_in = []
     for d in range(1, NY):
@@ -178,12 +179,17 @@
     own_d = pltpu.make_async_copy(decay_ref, dec.at[c], loc.at[4])
     own_d.start()
 
+    wsend(0, wl.at[opp, first_h], wtmp.at[0], {"col": right})
+    wsend(1, wl.at[opp, second_h], wtmp.at[1], {"col": left})
+    wsend(2, wl.at[right, mine_h], w.at[c, mine_h], {"col": right})
+    wsend(3, wl.at[left, mine_h], w.at[c, mine_h], {"col": left})
+    own_w = pltpu.make_async_copy(wl.at[c], w.at[c], loc.at[2])
+    own_w.start()
+
+    pl.semaphore_wait(side_sem, 1)
     for step in range(3):
-        pl.semaphore_signal(up_sem, inc=1, device_id=at_z(nz - 1), device_id_type=MESH)
-        pl.semaphore_signal(down_sem, inc=1, device_id=at_z(1), device_id_type=MESH)
-        if step == 0:
-            pl.semaphore_signal(side_sem, inc=1, device_id=at_x(NX - 1), device_id_type=MESH)
-            pl.semaphore_wait(side_sem, 1)
+        if step > 0:
+            greet()
         pl.semaphore_wait(up_sem, 1)
         pl.semaphore_wait(down_sem, 1)
 

time: 41.9 us -> 41.1 us (0.981)
  Pallas kernels: 40 us -> 39.3 us
    pallas_call x1, Pallas kernels: 40 us -> 39.3 us  [body(): pl.pallas_call(functools.partial(kernel, n_req), out_shape=jax.ShapeDtype...]
where the time goes in v5:
time: 41.1 us; the launch traced here: 41 us
  Pallas kernels  39.3 us (96%)
  local copies, waits for them, and re-layouts  1.67 us (4%)
    pallas_call x1, Pallas kernels, body(): pl.pallas_call(functools.partial(kernel, n_req), out_shape=jax.ShapeDtype...  39.3 us
    unnamed x1, local copies, waits for them, and re-layouts  1.67 us

profile of v5, /device:TPU:25, one launch (start us, length us, event | category | flops | bytes accessed | tf_op | source)
XLA Modules:
  0.0 41.0 jit_solution(12329748397943088989)
XLA Ops:
  0.0 39.3 %memory_layer.1 = bf16[256,512]{1,0:T(8,128)(2,1)} custom-call(s32[64]{0:T(128)} %row_ref.1, s32[2,32]{1,0:T(2,128)} %bitcast.4, s32[2,32]{1,0:T(2,128)} %bitcast.5, s32[64]{0:T(128)} %slot_ref.1, bf16[512,256]{1,0:T(8,128)(2,1)} %tok_ref.1, bf16[256,4,512]{2,1,0:T(4,128)(2,1)} %w_ref.1, bf16[2,16,1024]{2,1,0:T(8,128)(2,1)} %bitcast.3, ...), custom_call_target="tpu_custom_call" | custom-call | tf_op jit(solution)/shard_map/memory_layer/pallas_call | solution.py:430
  39.3 1.7 %copy.12 = bf16[256,512]{1,0:T(8,128)(2,1)} copy(bf16[256,512]{1,0:T(8,128)(2,1)} %memory_layer.1) | data formatting | bytes 524288
